TPU v7x, 32 devices: a whole 2x2x4 slice. The times are simulated.
32 devices in a mesh: aux: 8 (over z, x), occ: 4 (over y, core).
Axes of the slice: x: 2, y: 2, z: 4, core: 2. Of those that a mesh axis runs over, the one named last changes fastest.
Arguments:
- blocks: float32 [384, 8, 4096], P('aux', 'occ'), may hold values from -6 to 6
- pair_list: int32 [8, 8, 2], P('aux', 'occ'), may hold values from 0 to 15
- pair_count: int32 [8], P('aux'), may hold values from 2 to 8, as said below
- orbitals: float32 [128, 1024], replicated, may hold values from -0.001953125 to 0.001953125
Outputs:
- exchange: float32 [1024, 1024], P('aux', 'occ')
Inputs may be any that keep to these rules, and one draw needn't show every extreme that they name: `pair_list`: block indices of the kept pairs; pairs may repeat. `pair_count`: slots at or beyond an auxiliary block's count are padding and contribute nothing; some auxiliary block uses all 8 slots.
All inputs are finite; a program needn't handle non-finite values.
Results may differ from a plain program's by a relative error of at most 0.0003.
Values sent between devices are 32-bit elements; how exact they have to be, the bound alone decides.
A program may use at most 64 MiB of HBM per device.

v0:
```python
import jax
import jax.numpy as jnp
from jax import lax
from jax.sharding import PartitionSpec as P

NBF = 1024
BLK = 64


def per_device(blocks, pair_list, pair_count, orbitals):
    aux_rows = blocks.shape[0]
    slot_count = blocks.shape[1]
    orbital_count = orbitals.shape[0]
    n_blocks = NBF // BLK
    occ_devs = lax.axis_size("occ")
    positions = jnp.arange(n_blocks, dtype=jnp.int32)
    first_slot = lax.axis_index("occ") * slot_count
    live_slot = first_slot + jnp.arange(slot_count, dtype=jnp.int32) < pair_count[0]
    row_ids = jnp.where(live_slot, pair_list[0, :, 0], -1)
    col_onehot = (pair_list[0, :, 1][:, None] == positions[None, :]).astype(jnp.float32)
    coefficients = orbitals.reshape(orbital_count, n_blocks, BLK)
    picked_cols = jnp.einsum(
        "iNn,sN->sin", coefficients, col_onehot, precision=lax.Precision.HIGHEST
    )
    tile_data = blocks.reshape(aux_rows, slot_count, BLK, BLK)
    half_tiles = jnp.einsum(
        "qsmn,sin->isqm", tile_data, picked_cols, precision=lax.Precision.HIGHEST
    )
    arrived = lax.all_to_all(
        half_tiles.reshape(orbital_count, slot_count, aux_rows * BLK),
        "occ",
        split_axis=0,
        concat_axis=1,
        tiled=True,
    )
    every_ids = lax.all_gather(row_ids, "occ", axis=0, tiled=True)
    row_onehot = (every_ids[:, None] == positions[None, :]).astype(jnp.float32)
    owned_rows = arrived.reshape(orbital_count // occ_devs, slot_count * occ_devs, aux_rows, BLK)
    transformed = jnp.einsum(
        "isqm,sM->iqMm", owned_rows, row_onehot, precision=lax.Precision.HIGHEST
    )
    transformed = transformed.reshape(orbital_count // occ_devs * aux_rows, NBF)
    partial_value = jnp.einsum(
        "rm,rn->mn", transformed, transformed, precision=lax.Precision.HIGHEST
    )
    by_row = lax.psum_scatter(partial_value, "aux", scatter_dimension=0, tiled=True)
    result = lax.psum_scatter(by_row, "occ", scatter_dimension=1, tiled=True)
    return result


def solution(mesh):
    in_specs = (P("aux", "occ", None), P("aux", "occ", None), P("aux"), P())
    out_specs = P("aux", "occ")
    return jax.shard_map(
        per_device, mesh=mesh, in_specs=in_specs, out_specs=out_specs, check_vma=False
    )
```

profile of v0, /device:TPU:0, one launch (start us, length us, event | category | flops | bytes accessed | tf_op | source)
XLA Modules:
  0.0 240.6 jit_solution(9319552325716334245)
XLA Ops:
  6.5 1.0 slice_reduce_fusion.1
  7.5 2.0 copy.11
  9.5 3.0 %reshape.19 = f32[48,2,64,64]{3,2,1,0:T(8,128)S(1)} reshape(f32[48,2,4096]{2,1,0:T(2,128)} %param.4) | data formatting | bytes 3145728 | tf_op jit(solution)/shard_map/reshape | solution.py:25
  12.6 1.6 convolution_bitcast_fusion
  14.2 4.4 %fusion.5 = f32[2,128,48,64]{1,3,2,0:T(8,128)} fusion(f32[48,2,64,64]{3,2,1,0:T(8,128)S(1)} %reshape.19, f32[2,128,64,1]{1,0,2,3:T(2,128)S(1)} %convolution_bitcast_fusion), kind=kOutput, calls=%fused_computation.3 | convolution fusion | flops 603979776 | bytes 4784128 | tf_op jit(solution)/shard_map/qsmn,sin->isqm/dot_general | solution.py:26
  18.6 5.9 %copy.15 = f32[128,2,3072]{2,1,0:T(2,128)} copy(f32[128,2,3072]{0,2,1:T(8,128)} %bitcast.30) | data formatting | bytes 6291456 | tf_op jit(solution)/shard_map/reshape | solution.py:30
  24.5 0.0 copy-start
  24.5 4.4 %all-to-all-start = ((f32[128,2,3072]{2,1,0:T(2,128)}), f32[128,2,3072]{2,1,0:T(2,128)S(1)}, u32[]{:S(2)}, u32[]{:S(2)}) async-start(f32[128,2,3072]{2,1,0:T(2,128)} %copy.15), calls=%async_computation | async-start | bytes 6291456 | tf_op jit(solution)/shard_map/all_to_all | solution.py:29
  28.9 0.0 reduce-scatter.3.cloned.1.call-start
  29.5 0.0 copy-done
  29.5 0.6 dynamic-slice
  30.8 0.1 fusion.15
  30.9 35.1 %all-reduce = s32[8]{0:T(128)S(1)} all-reduce(s32[8]{0:T(128)S(1)} %fusion.15), channel_id=1, replica_groups=mesh['aux'=8,'occ'=4] {'occ'}, use_global_device_ids=true, to_apply=%add | all-reduce | flops 8 | bytes 64
  66.0 0.0 all-to-all-done
  66.0 1.0 copy.16
  67.0 0.2 copy.17
  67.2 3.7 %reshape.21 = f32[32,8,48,64]{3,2,0,1:T(8,128)} reshape(f32[32,4,2,3072]{3,0,2,1:T(8,128)S(1)} %copy.17) | data formatting | bytes 6291456 | tf_op jit(solution)/shard_map/reshape | solution.py:38
  70.9 12.9 %fusion.2 = f32[32,48,16,64]{3,2,1,0:T(8,128)} fusion(f32[32,8,48,64]{3,2,0,1:T(8,128)} %reshape.21, s32[8]{0:T(128)S(1)} %all-reduce), kind=kOutput, calls=%fused_computation.2 | convolution fusion | flops 150995072 | bytes 9437216 | tf_op jit(solution)/shard_map/isqm,sM->iqMm/dot_general | solution.py:39
  83.8 11.6 %reshape.22 = f32[1536,1024]{1,0:T(8,128)} reshape(f32[32,48,16,64]{3,2,1,0:T(8,128)} %fusion.2) | data formatting | bytes 12582912 | tf_op jit(solution)/shard_map/reshape | solution.py:42
  95.4 25.0 %fusion.17 = f32[1024,1024]{1,0:T(8,128)} fusion(f32[1536,1024]{1,0:T(8,128)} %reshape.22), kind=kOutput, calls=%fused_computation.19 | convolution fusion | flops 19327352832 | bytes 10485760 | tf_op jit(solution)/shard_map/rm,rn->mn/dot_general | solution.py:43
  120.4 0.0 reduce-scatter.3.cloned.1.call-update
  120.4 0.0 reduce-scatter.5.cloned.1.call-start
  120.5 89.5 %reduce-scatter.3.cloned.1.call-done = f32[128,1024]{1,0:T(8,128)} async-done(((f32[1024,1024]{1,0:T(8,128)}), f32[128,1024]{1,0:T(8,128)}) %reduce-scatter.3.cloned.1.call-update) | async-done | bytes 524304 | tf_op jit(solution)/shard_map/reduce_scatter | solution.py:46
  210.0 0.0 reduce-scatter.5.cloned.1.call-update
  210.0 23.8 %reduce-scatter.5.cloned.1.call-done = f32[128,256]{1,0:T(8,128)} async-done(((f32[128,1024]{1,0:T(8,128)}), f32[128,256]{1,0:T(8,128)}) %reduce-scatter.5.cloned.1.call-update) | async-done | bytes 131088 | tf_op jit(solution)/shard_map/reduce_scatter | solution.py:47
  (1 shorter events, 0.0 us)
Async XLA Ops:
  24.5 5.0 %copy-start = (u32[32]{0:T(128)S(1)}, u32[32]{0:T(128)}, u32[]{:S(2)}) copy-start(u32[32]{0:T(128)} %constant.13) | copy-start | bytes 388
  24.5 41.5 %all-to-all-start = ((f32[128,2,3072]{2,1,0:T(2,128)}), f32[128,2,3072]{2,1,0:T(2,128)S(1)}, u32[]{:S(2)}, u32[]{:S(2)}) async-start(f32[128,2,3072]{2,1,0:T(2,128)} %copy.15), calls=%async_computation | async-start | bytes 6291456 | tf_op jit(solution)/shard_map/all_to_all | solution.py:29
  28.9 181.1 %reduce-scatter.3.cloned.1.call-start = ((), (), s32[]{:S(2)}) async-start(), calls=%async_computation.3 | async-start | bytes 4718592 | tf_op jit(solution)/shard_map/reduce_scatter | solution.py:46
  120.4 113.3 %reduce-scatter.5.cloned.1.call-start = ((), (), s32[]{:S(2)}) async-start(), calls=%async_computation.4 | async-start | bytes 655360 | tf_op jit(solution)/shard_map/reduce_scatter | solution.py:47
Sparse Core Ops, SparseCore 0:
  120.6 89.3 reduce-scatter.2
  212.5 21.2 reduce-scatter.4
where the time goes:
time: 241 us
  waiting for transfers between devices  113 us (47%)
  matrix products  43.9 us (18%)
  blocking collectives  35.1 us (15%)
  local copies, waits for them, and re-layouts  29 us (12%)
  between operations  14.8 us (6%)
  starting transfers between devices  4.43 us (2%)
    reduce_scatter x1, waiting for transfers between devices, per_device(): lax.psum_scatter(partial_value, 'aux', scatter_dimension=0, tiled=True)  89.5 us
    unnamed x1, blocking collectives  35.1 us
    dot_general x1, matrix products, per_device(): jnp.einsum('rm,rn->mn', transformed, transformed, precision=lax.Precision...  25 us
    reduce_scatter x1, waiting for transfers between devices, per_device(): result = lax.psum_scatter(by_row, 'occ', scatter_dimension=1, tiled=True)  23.8 us
    dot_general x1, matrix products, per_device(): jnp.einsum('isqm,sM->iqMm', owned_rows, row_onehot, precision=lax.Precisi...  12.9 us
    reshape x1, local copies, waits for them, and re-layouts, per_device(): transformed = transformed.reshape(orbital_count // occ_devs * aux_rows, NBF)  11.6 us
    reshape x1, local copies, waits for them, and re-layouts, per_device(): half_tiles.reshape(orbital_count, slot_count, aux_rows * BLK)  5.86 us
  transfers between devices with their start and end apart: 3, of which 2 were waited for; matrix products, arithmetic and copies ran while one was open for 0% of the time, Pallas kernels for 0%

commit v1 on v0

v1 whole, which is shorter than its diff:
```python
import functools

import jax
import jax.numpy as jnp
from jax import lax
from jax.experimental import pallas as pl
from jax.experimental.pallas import tpu as pltpu
from jax.sharding import PartitionSpec as P

LANES = 128
SIDE = 256
MESH = pl.DeviceIdType.MESH
NT = (((1,), (1,)), ((), ()))
NN = (((1,), (0,)), ((), ()))


def dot(a, b, dims):
    return lax.dot_general(a, b, dims, preferred_element_type=jnp.float32)


def split(x):
    hi = x.astype(jnp.bfloat16)
    return hi, (x - hi.astype(jnp.float32)).astype(jnp.bfloat16)


def kernel(n_aux, n_occ, n_sub, tiles, info, orb, out, rx, ids, whi, wlo, hhi, hlo, part, core_in,
           pair, y_in, full, dense, z_in, local_sem, tile_s, tile_r, ids_s, ids_r, idx_s, idx_r,
           core_s, core_r, ys_s, ys_r, gy_s, gy_r, gx_s, gx_r, fy_s, fy_r, gc_s, gc_r, z_s, z_r):
    a, o = lax.axis_index("aux"), lax.axis_index("occ")
    n_y, n_hi = n_occ // 2, n_aux // 2
    y, c = o // 2, lax.rem(o, 2)
    hi_a, lo = a // 2, lax.rem(a, 2)
    own_q = tiles.shape[0] // n_occ
    sub_q = own_q // n_sub
    krows = tiles.shape[1] // 2
    n_slots = 2 * n_occ
    n_side = n_slots * 2 * krows // SIDE
    total_rows = part.shape[0]
    half_rows, quarter = total_rows // 2, total_rows // n_occ

    def occ_peer(dy, dc):
        return lax.rem(y + dy, n_y) * 2 + (c if dc == 0 else 1 - c)

    peers = [(dy, dc) for dy in range(1, n_y) for dc in (0, 1)] + [(0, 1)]
    partner = (a, occ_peer(0, 1))
    x_peer = (a + 1 - 2 * lo, o)

    def z_peer(d):
        return (lax.rem(hi_a + d, n_hi) * 2 + lo, o)

    barrier = pltpu.get_barrier_semaphore()
    greet = [(a, occ_peer(*d)) for d in peers] + [x_peer] + [z_peer(d) for d in range(1, n_hi)]
    for dev in greet:
        pl.semaphore_signal(barrier, inc=1, device_id=dev, device_id_type=MESH)
    ids[lo, o] = info[...]
    own = pltpu.make_async_copy(tiles.at[pl.ds(o * own_q, own_q)], rx.at[o], local_sem)
    own.start()
    pl.semaphore_wait(barrier, len(greet))

    def remote(src, dst, s, r, dev):
        cp = pltpu.make_async_remote_copy(
            src_ref=src, dst_ref=dst, send_sem=s, recv_sem=r, device_id=dev, device_id_type=MESH
        )
        cp.start()
        return cp

    id_copies = []
    for d, (dy, dc) in enumerate(peers):
        id_copies.append(remote(info, ids.at[lo, o], ids_s.at[d], ids_r.at[d], (a, occ_peer(dy, dc))))
    tile_copies = []
    for j in range(n_sub):
        row = []
        for d, (dy, dc) in enumerate(peers):
            peer = occ_peer(dy, dc)
            row.append(remote(
                tiles.at[pl.ds(peer * own_q + j * sub_q, sub_q)],
                rx.at[o, pl.ds(j * sub_q, sub_q)],
                tile_s.at[j, d], tile_r.at[j, d], (a, peer)))
        tile_copies.append(row)
    for cp in id_copies:
        cp.wait()
    idx_copy = remote(ids.at[lo], ids.at[lo], idx_s, idx_r, x_peer)

    nbf, n_orb = orb.shape[1], orb.shape[0]
    orb_hi, orb_lo = split(orb[...])
    row_pos = lax.broadcasted_iota(jnp.int32, (nbf, LANES), 0)
    lane = lax.broadcasted_iota(jnp.int32, (n_orb, LANES), 1)
    for s in range(n_slots):
        sel = (row_pos == ids[lo, s // 2, pl.ds(s % 2, 1), :]).astype(jnp.float32).astype(jnp.bfloat16)
        for src, dst in ((orb_hi, whi), (orb_lo, wlo)):
            w = dot(src, sel, NN)
            dst[s, 0:n_orb, :] = jnp.where(lane < LANES // 2, w, 0.0).astype(jnp.bfloat16)
            dst[s, n_orb:2 * n_orb, :] = jnp.where(lane >= LANES // 2, w, 0.0).astype(jnp.bfloat16)

    own.wait()
    pairs = [(i, j) for i in range(n_side) for j in range(i + 1)]
    for j in range(n_sub):
        for cp in tile_copies[j]:
            cp.wait()
        for s in range(n_slots):
            rows = jnp.concatenate(
                [rx[s // 2, j * sub_q + q, pl.ds(s % 2, krows, stride=2), :] for q in range(sub_q)], axis=0)
            bh, bl = split(rows)
            res = dot(bh, whi[s], NT) + dot(bl, whi[s], NT) + dot(bh, wlo[s], NT)
            for q in range(sub_q):
                for p in range(2):
                    piece = res[q * krows:(q + 1) * krows, p * n_orb:(p + 1) * n_orb]
                    ph, pl_ = split(piece)
                    r0 = (2 * s + p) * krows
                    hhi[r0:r0 + krows, q * n_orb:(q + 1) * n_orb] = ph
                    hlo[r0:r0 + krows, q * n_orb:(q + 1) * n_orb] = pl_
        for b, (i, k) in enumerate(pairs):
            ih, il = hhi[i * SIDE:(i + 1) * SIDE, :], hlo[i * SIDE:(i + 1) * SIDE, :]
            kh, kl = hhi[k * SIDE:(k + 1) * SIDE, :], hlo[k * SIDE:(k + 1) * SIDE, :]
            val = dot(ih, kh, NT) + dot(ih, kl, NT) + dot(il, kh, NT)
            if j:
                val = val + part[b * SIDE:(b + 1) * SIDE, :]
            part[b * SIDE:(b + 1) * SIDE, :] = val

    cp = remote(part.at[pl.ds((1 - c) * half_rows, half_rows)], core_in, core_s, core_r, partner)
    cp.wait()
    pair[...] = part[pl.ds(pl.multiple_of(c * half_rows, 8), half_rows), :] + core_in[...]
    copies = []
    for d in range(1, n_y):
        dev_y = lax.rem(y + d, n_y)
        copies.append(remote(pair.at[pl.ds(dev_y * quarter, quarter)], y_in.at[d - 1],
                             ys_s.at[d - 1], ys_r.at[d - 1], (a, dev_y * 2 + c)))
    total = pair[pl.ds(pl.multiple_of(y * quarter, 8), quarter), :]
    for d in range(1, n_y):
        copies[d - 1].wait()
        total = total + y_in[d - 1]
    at = o_row = c * half_rows + y * quarter
    full[lo, pl.ds(pl.multiple_of(at, 8), quarter), :] = total
    mine = full.at[lo, pl.ds(o_row, quarter)]
    gx = remote(mine, mine, gx_s, gx_r, x_peer)
    gys = []
    for d in range(1, n_y):
        gys.append(remote(mine, mine, gy_s.at[d - 1], gy_r.at[d - 1],
                          (a, lax.rem(y + d, n_y) * 2 + c)))
    gx.wait()
    other = full.at[1 - lo, pl.ds(o_row, quarter)]
    fys = []
    for d in range(1, n_y):
        fys.append(remote(other, other, fy_s.at[d - 1], fy_r.at[d - 1],
                          (a, lax.rem(y + d, n_y) * 2 + c)))
    for cp in gys:
        cp.wait()
    mine_half = full.at[lo, pl.ds(c * half_rows, half_rows)]
    gc0 = remote(mine_half, mine_half, gc_s.at[0], gc_r.at[0], partner)
    for cp in fys:
        cp.wait()
    other_half = full.at[1 - lo, pl.ds(c * half_rows, half_rows)]
    gc1 = remote(other_half, other_half, gc_s.at[1], gc_r.at[1], partner)
    idx_copy.wait()
    gc0.wait()
    gc1.wait()

    out_rows, out_cols = out.shape
    compact = n_slots * 2 * krows
    col_pos = lax.broadcasted_iota(jnp.int32, (out_cols, compact), 0) + o * out_cols
    row_i = lax.broadcasted_iota(jnp.int32, (n_hi * out_rows, compact), 0)
    row_pos = (row_i // out_rows * 2 + lo) * out_rows + lax.rem(row_i, out_rows)
    acc = None
    for l in range(2):
        where = jnp.concatenate([ids[l, s, 2:3, :] for s in range(n_occ)], axis=1)
        cols = (col_pos == where).astype(jnp.float32).astype(jnp.bfloat16)
        rows = (row_pos == where).astype(jnp.float32).astype(jnp.bfloat16)
        t = [None] * n_side

        def add(i, v):
            t[i] = v if t[i] is None else t[i] + v

        for b, (i, k) in enumerate(pairs):
            for e in split(full[l, b * SIDE:(b + 1) * SIDE, :]):
                add(i, dot(e, cols[:, k * SIDE:(k + 1) * SIDE], NT))
                if i != k:
                    add(k, lax.dot_general(e, cols[:, i * SIDE:(i + 1) * SIDE], (((0,), (1,)), ((), ())),
                                           preferred_element_type=jnp.float32))
        for i in range(n_side):
            for e in split(t[i]):
                v = dot(rows[:, i * SIDE:(i + 1) * SIDE], e, NN)
                acc = v if acc is None else acc + v
    for h in range(n_hi):
        dense[h] = acc[h * out_rows:(h + 1) * out_rows, :]
    zs = []
    for d in range(1, n_hi):
        zs.append(remote(dense.at[lax.rem(hi_a + d, n_hi)], z_in.at[d - 1],
                         z_s.at[d - 1], z_r.at[d - 1], z_peer(d)))
    result = dense[hi_a]
    for d in range(1, n_hi):
        zs[d - 1].wait()
        result = result + z_in[d - 1]
    out[...] = result


def per_device(n_aux, n_occ, blocks, pair_list, pair_count, orbitals):
    n_q, slots, area = blocks.shape
    n_orb, nbf = orbitals.shape
    krows = area // LANES
    blk = LANES // 2
    tiles = blocks.reshape(n_q, slots, krows, LANES).transpose(0, 2, 1, 3).reshape(n_q, krows * slots, LANES)
    first = lax.axis_index("occ") * slots
    live = first + jnp.arange(slots, dtype=jnp.int32) < pair_count[0]
    lane = jnp.arange(LANES, dtype=jnp.int32)
    col_of = pair_list[0, :, 1][:, None] * blk + (lane % blk)[None, :]
    in_row = jnp.arange(blk, dtype=jnp.int32)
    in_row = in_row % krows * 2 + in_row // krows
    row_of = jnp.where(live[:, None], pair_list[0, :, 0][:, None] * blk + in_row[None, :], -1)
    info = jnp.concatenate([col_of, row_of.reshape(1, slots * blk), jnp.zeros((5, LANES), jnp.int32)], axis=0)

    own_q = n_q // n_occ
    n_sub = 3
    compact = slots * n_occ * blk
    n_side = compact // SIDE
    total_rows = n_side * (n_side + 1) // 2 * SIDE
    half, quarter = total_rows // 2, total_rows // n_occ
    n_y, n_hi = n_occ // 2, n_aux // 2
    out_rows, out_cols = nbf // n_aux, nbf // n_occ
    f32, bf16, dma = jnp.float32, jnp.bfloat16, pltpu.SemaphoreType.DMA
    return pl.pallas_call(
        functools.partial(kernel, n_aux, n_occ, n_sub),
        name="exchange",
        out_shape=jax.ShapeDtypeStruct((out_rows, out_cols), f32),
        in_specs=[pl.BlockSpec(memory_space=pl.ANY)] + [pl.BlockSpec(memory_space=pltpu.VMEM)] * 2,
        out_specs=pl.BlockSpec(memory_space=pltpu.VMEM),
        scratch_shapes=[
            pltpu.VMEM((n_occ, own_q, krows * slots, LANES), f32),
            pltpu.VMEM((2, n_occ, 8, LANES), jnp.int32),
            pltpu.VMEM((slots * n_occ, 2 * n_orb, LANES), bf16),
            pltpu.VMEM((slots * n_occ, 2 * n_orb, LANES), bf16),
            pltpu.VMEM((compact, own_q // n_sub * n_orb), bf16),
            pltpu.VMEM((compact, own_q // n_sub * n_orb), bf16),
            pltpu.VMEM((total_rows, SIDE), f32),
            pltpu.VMEM((half, SIDE), f32),
            pltpu.VMEM((half, SIDE), f32),
            pltpu.VMEM((n_y - 1, quarter, SIDE), f32),
            pltpu.VMEM((2, total_rows, SIDE), f32),
            pltpu.VMEM((n_hi, out_rows, out_cols), f32),
            pltpu.VMEM((n_hi - 1, out_rows, out_cols), f32),
            dma,
            dma((n_sub, n_occ - 1)), dma((n_sub, n_occ - 1)),
            dma((n_occ - 1,)), dma((n_occ - 1,)),
            dma, dma,
            dma, dma,
            dma((n_y - 1,)), dma((n_y - 1,)),
            dma((n_y - 1,)), dma((n_y - 1,)),
            dma, dma,
            dma((n_y - 1,)), dma((n_y - 1,)),
            dma((2,)), dma((2,)),
            dma((n_hi - 1,)), dma((n_hi - 1,)),
        ],
        compiler_params=pltpu.CompilerParams(collective_id=0, has_side_effects=True),
    )(tiles, info, orbitals)


def solution(mesh):
    body = functools.partial(per_device, mesh.shape["aux"], mesh.shape["occ"])
    in_specs = (P("aux", "occ", None), P("aux", "occ", None), P("aux"), P())
    return jax.shard_map(body, mesh=mesh, in_specs=in_specs, out_specs=P("aux", "occ"), check_vma=False)
```

time: 241 us -> 64.6 us (0.27)
  waiting for transfers between devices: 113 us -> 0 us
  Pallas kernels: 0 us -> 60.2 us
  matrix products: 43.9 us -> 0 us
  blocking collectives: 35.1 us -> 0 us
  local copies, waits for them, and re-layouts: 29 us -> 1.73 us
  between operations: 14.8 us -> 0.68 us
  starting transfers between devices: 4.43 us -> 0 us
    reduce_scatter x2 -> x0, waiting for transfers between devices: 113 us -> none  [the longest x1 89.5 us: per_device(): lax.psum_scatter(partial_value, 'aux', scatter_dimension=0, tiled=True)]
    pallas_call x0 -> x1, Pallas kernels: none -> 60.2 us  [per_device(): pl.pallas_call(functools.partial(kernel, n_aux, n_occ, n_sub), name='exch...]
    dot_general x4 -> x0, matrix products: 43.9 us -> none  [the longest x1 25 us: per_device(): jnp.einsum('rm,rn->mn', transformed, transformed, precision=lax.Precision...]
    unnamed x1 -> x0, blocking collectives: 35.1 us -> none
    reshape x4 -> x0, local copies, waits for them, and re-layouts: 24.2 us -> none  [the longest x1 11.6 us: per_device(): transformed = transformed.reshape(orbital_count // occ_devs * aux_rows, NBF)]
    all_to_all x1 -> x0, starting transfers between devices: 4.39 us -> none  [per_device(): lax.all_to_all(half_tiles.reshape(orbital_count, slot_count, aux_rows * B...]
  transfers between devices with their start and end apart: 3 -> 0, of which waited for: 2 -> 0; matrix products, arithmetic and copies ran while one was open for 0% -> 0% of each run, Pallas kernels for 0% -> 0%
where the time goes in v1:
time: 64.6 us; the launch traced here: 64.4 us
  Pallas kernels  60.2 us (93%)
  other arithmetic  1.79 us (3%)
  local copies, waits for them, and re-layouts  1.73 us (3%)
  between operations  0.68 us (1%)
    pallas_call x1, Pallas kernels, per_device(): pl.pallas_call(functools.partial(kernel, n_aux, n_occ, n_sub), name='exch...  60.2 us
    unnamed x1, local copies, waits for them, and re-layouts  1.57 us

profile of v1, /device:TPU:0, one launch (start us, length us, event | category | flops | bytes accessed | tf_op | source)
XLA Modules:
  0.0 64.4 jit_solution(6083678310800990595)
XLA Ops:
  0.7 0.1 pad.2.clone
  0.8 1.0 %multiply_reduce_fusion.1 = (s32[2]{0:T(128)S(1)}, s32[2]{0:T(128)S(1)}) fusion(s32[1,2,2]{2,1,0:T(2,128)} %param.5), kind=kLoop, calls=%fused_computation.9 | loop fusion | flops 4 | bytes 32 | tf_op jit(solution)/shard_map/mul | solution.py:205
  1.7 0.1 broadcast_add_fusion
  1.8 0.1 add_select_fusion
  1.9 0.1 select_n.48
  2.0 0.7 %add_add_fusion.info = s32[8,128]{1,0:T(8,128)} fusion(s32[1,128]{1,0:T(1,128)S(1)} %select_n.48, s32[2,128]{1,0:T(2,128)S(1)} %broadcast_add_fusion, s32[8]{0:T(128)S(1)} %pad.2.clone), kind=kLoop, calls=%fused_computation | loop fusion | flops 2048 | bytes 5664 | tf_op jit(solution)/shard_map/concatenate | solution.py:209
  2.6 60.2 %exchange.1 = f32[128,256]{1,0:T(8,128)} custom-call(f32[48,64,128]{2,1,0:T(8,128)} %bitcast.7, s32[8,128]{1,0:T(8,128)} %add_add_fusion.info, f32[128,1024]{1,0:T(8,128)} %orb.1), custom_call_target="tpu_custom_call" | custom-call | tf_op jit(solution)/shard_map/exchange/pallas_call | solution.py:220
  62.8 1.6 %copy.8 = f32[128,256]{1,0:T(8,128)} copy(f32[128,256]{1,0:T(8,128)} %exchange.1) | data formatting | bytes 262144
  (4 shorter events, 0.0 us)

commit v2 on v0

v2 whole, which is shorter than its diff:
```python
import functools

import jax
import jax.numpy as jnp
from jax import lax
from jax.experimental import pallas as pl
from jax.experimental.pallas import tpu as pltpu
from jax.sharding import PartitionSpec as P

LANES = 128
PIECES = 2
MESH = pl.DeviceIdType.MESH
NT = (((1,), (1,)), ((), ()))
NN = (((1,), (0,)), ((), ()))


def dot(a, b, dims):
    return lax.dot_general(a, b, dims, preferred_element_type=jnp.float32)


def split(x):
    hi = x.astype(jnp.bfloat16)
    return hi, (x - hi.astype(jnp.float32)).astype(jnp.bfloat16)


def kernel(n_aux, n_occ, n_sub, tiles, pairs_in, count_in, orb, out, rx, rxd, ids, whi, wlo, hhi, hlo,
           dhi, dlo, diag, dcore, dfull, off, ocore, opair, oin, ofull, dense, z_in,
           local_s, tile_s, tile_r, quart_s, quart_r, ids_s, ids_r, idx_s, idx_r, dc_s, dc_r,
           dx_s, dx_r, dy_s, dy_r, df_s, df_r, dd_s, dd_r, oc_s, oc_r, oy_s, oy_r, ox_s, ox_r,
           op_s, op_r, of_s, of_r, z_s, z_r):
    a, o = lax.axis_index("aux"), lax.axis_index("occ")
    n_y, n_hi = n_occ // 2, n_aux // 2
    y, c = o // 2, lax.rem(o, 2)
    hi_a, lo = a // 2, lax.rem(a, 2)
    own_q = tiles.shape[0] // n_occ
    sub_q = own_q // n_sub
    krows = tiles.shape[1] // 2
    blk = 2 * krows
    side = 4 * blk
    n_slots = 2 * n_occ
    n_off = n_y * (n_y - 1) // 2
    d_half, o_half = side // 2, n_off * side // 2
    piece = o_half // PIECES
    nbf, n_orb = orb.shape[1], orb.shape[0]

    def y_peer(d):
        return lax.rem(y + d, n_y)

    peers = [(d, e) for d in range(1, n_y) for e in (0, 1)] + [(0, 1)]

    def occ_peer(d, e):
        return y_peer(d) * 2 + (c if e == 0 else 1 - c)

    partner = (a, occ_peer(0, 1))
    x_peer = (a + 1 - 2 * lo, o)

    def z_peer(d):
        return (lax.rem(hi_a + d, n_hi) * 2 + lo, o)

    barrier = pltpu.get_barrier_semaphore()
    greet = [(a, occ_peer(*d)) for d in peers] + [x_peer] + [z_peer(d) for d in range(1, n_hi)]
    for dev in greet:
        pl.semaphore_signal(barrier, inc=1, device_id=dev, device_id_type=MESH)

    def local(src, dst, s):
        cp = pltpu.make_async_copy(src, dst, s)
        cp.start()
        return cp

    def quarter(index):
        return tiles.at[pl.ds(index * own_q, own_q)]

    locals_ = [local(quarter(o), rx.at[o], local_s.at[0])]
    for d in range(1, n_y):
        locals_.append(local(quarter(y_peer(d) * 2 + c), rxd.at[c, d - 1], local_s.at[d]))
    lane1 = lax.broadcasted_iota(jnp.int32, (8, LANES), 1)
    row1 = lax.broadcasted_iota(jnp.int32, (8, LANES), 0)
    within = lax.rem(lane1, blk)
    place = lax.rem(within, krows) * 2 + within // krows
    live = [jnp.where(o * 2 + s < count_in[0], pairs_in[0, s, 0] * blk, -nbf - blk) for s in range(2)]
    cols = jnp.where(row1 == 0, pairs_in[0, 0, 1], pairs_in[0, 1, 1]) * blk + within
    ids[lo, o] = jnp.where(row1 < 2, cols, jnp.where(lane1 < blk, live[0], live[1]) + place)
    pl.semaphore_wait(barrier, len(greet))

    def remote(src, dst, s, r, dev):
        cp = pltpu.make_async_remote_copy(
            src_ref=src, dst_ref=dst, send_sem=s, recv_sem=r, device_id=dev, device_id_type=MESH
        )
        cp.start()
        return cp

    def sub_tiles(j, d, e):
        peer = occ_peer(d, e)
        n = d * 2 + e
        return remote(tiles.at[pl.ds(peer * own_q + j * sub_q, sub_q)], rx.at[o, pl.ds(j * sub_q, sub_q)],
                      tile_s.at[j, n], tile_r.at[j, n], (a, peer))

    id_copies = []
    for n, d in enumerate(peers):
        id_copies.append(remote(ids.at[lo, o], ids.at[lo, o], ids_s.at[n], ids_r.at[n], (a, occ_peer(*d))))
    tile_copies = [[sub_tiles(j, d, e) for d in range(1, n_y) for e in (0, 1)] for j in range(n_sub)]
    quarters = []
    for d in range(1, n_y):
        quarters.append(remote(quarter(y_peer(d) * 2 + 1 - c), rxd.at[c, d - 1],
                               quart_s.at[d], quart_r.at[d], partner))
    quarters.append(remote(quarter(o + 1 - 2 * c), rx.at[o], quart_s.at[0], quart_r.at[0], partner))

    orb_hi, orb_lo = split(orb[...])
    row_pos = lax.broadcasted_iota(jnp.int32, (nbf, LANES), 0)
    lane = lax.broadcasted_iota(jnp.int32, (n_orb, LANES), 1)
    for cp in id_copies:
        cp.wait()
    idx_copy = remote(ids.at[lo], ids.at[lo], idx_s, idx_r, x_peer)
    for s in range(n_slots):
        sel = (row_pos == ids[lo, s // 2, pl.ds(s % 2, 1), :]).astype(jnp.float32)
        sel = sel.astype(jnp.bfloat16)
        for src, dst in ((orb_hi, whi), (orb_lo, wlo)):
            w = dot(src, sel, NN)
            dst[s, 0:n_orb, :] = jnp.where(lane < blk, w, 0.0).astype(jnp.bfloat16)
            dst[s, n_orb:2 * n_orb, :] = jnp.where(lane >= blk, w, 0.0).astype(jnp.bfloat16)

    def half(load, slot, row0, q0, hi_ref, lo_ref):
        rows = jnp.concatenate([load(q) for q in range(sub_q)], axis=0)
        bh, bl = split(rows)
        wh, wl = whi[slot], wlo[slot]
        res = dot(bh, wh, NT) + dot(bl, wh, NT) + dot(bh, wl, NT)
        for q in range(sub_q):
            for p in range(2):
                ph, pl_ = split(res[q * krows:(q + 1) * krows, p * n_orb:(p + 1) * n_orb])
                at = pl.ds(pl.multiple_of(row0 + p * krows, krows), krows)
                lanes = slice((q0 + q) * n_orb, (q0 + q + 1) * n_orb)
                hi_ref[at, lanes] = ph
                lo_ref[at, lanes] = pl_

    def gram(hi_i, lo_i, hi_k, lo_k):
        return dot(hi_i, hi_k, NT) + dot(hi_i, lo_k, NT) + dot(lo_i, hi_k, NT)

    for cp in locals_ + quarters:
        cp.wait()
    total = None
    for d in range(1, n_y):
        for j in range(n_sub):
            for e in range(2):
                for s in range(2):
                    half(lambda q: rxd[e, d - 1, j * sub_q + q, pl.ds(s, krows, stride=2), :],
                         (y * 2 + e) * 2 + s, (e * 2 + s) * blk, 0, dhi, dlo)
            val = gram(dhi[...], dlo[...], dhi[...], dlo[...])
            total = val if total is None else total + val
    mine = pl.ds(pl.multiple_of(y * side, side), side)
    for j in range(n_sub):
        for e in range(2):
            for s in range(2):
                half(lambda q: rx[y * 2 + e, j * sub_q + q, pl.ds(s, krows, stride=2), :],
                     (y * 2 + e) * 2 + s, ((y * 2 + e) * 2 + s) * blk, j * sub_q, hhi, hlo)
    total = total + gram(hhi[mine, :], hlo[mine, :], hhi[mine, :], hlo[mine, :])
    diag[...] = total
    cp = remote(diag.at[pl.ds((1 - c) * d_half, d_half)], dcore, dc_s, dc_r, partner)
    cp.wait()
    my_d = pl.ds(pl.multiple_of(c * d_half, d_half), d_half)
    dfull[lo, y, my_d, :] = diag[my_d, :] + dcore[...]
    my_diag = dfull.at[lo, y, my_d]
    dx = [remote(my_diag, my_diag, dx_s, dx_r, x_peer)]
    dys = [remote(my_diag, my_diag, dy_s.at[d], dy_r.at[d], (a, y_peer(d) * 2 + c)) for d in range(1, n_y)]

    offs = [(i, k) for i in range(n_y) for k in range(i)]
    for j in range(n_sub):
        for cp in tile_copies[j]:
            cp.wait()
        for d in range(1, n_y):
            for e in range(2):
                for s in range(2):
                    src = y_peer(d) * 2 + e
                    half(lambda q: rx[src, j * sub_q + q, pl.ds(s, krows, stride=2), :],
                         src * 2 + s, (src * 2 + s) * blk, j * sub_q, hhi, hlo)
        at = slice(j * sub_q * n_orb, (j + 1) * sub_q * n_orb)
        for b, (i, k) in enumerate(offs):
            ri, rk = slice(i * side, (i + 1) * side), slice(k * side, (k + 1) * side)
            val = gram(hhi[ri, at], hlo[ri, at], hhi[rk, at], hlo[rk, at])
            if j:
                val = val + off[b * side:(b + 1) * side, :]
            off[b * side:(b + 1) * side, :] = val
    cp = remote(off.at[pl.ds((1 - c) * o_half, o_half)], ocore, oc_s, oc_r, partner)
    cp.wait()
    opair[...] = off[pl.ds(pl.multiple_of(c * o_half, piece), o_half), :] + ocore[...]
    oys = []
    for p in range(PIECES):
        at = pl.ds(p * piece, piece)
        oys.append([remote(opair.at[at], oin.at[d - 1, at], oy_s.at[p, d - 1], oy_r.at[p, d - 1],
                           (a, y_peer(d) * 2 + c)) for d in range(1, n_y)])
    dfs = []
    for d in range(1, n_y):
        dys[d - 1].wait_recv()
        got = dfull.at[lo, y_peer(n_y - d), my_d]
        dfs.append(remote(got, got, df_s.at[d], df_r.at[d], x_peer))
    oxs, ops = [], []
    for p in range(PIECES):
        val = opair[p * piece:(p + 1) * piece, :]
        for d in range(1, n_y):
            oys[p][d - 1].wait()
            val = val + oin[d - 1, p * piece:(p + 1) * piece, :]
        at = pl.ds(pl.multiple_of(c * o_half + p * piece, piece), piece)
        ofull[lo, at, :] = val
        ref = ofull.at[lo, at]
        oxs.append(remote(ref, ref, ox_s.at[p], ox_r.at[p], x_peer))
        ops.append(remote(ref, ref, op_s.at[p], op_r.at[p], partner))
    for cp in dx + dfs:
        cp.wait()
    for cp in dys:
        cp.wait_send()
    idx_copy.wait()
    half_d = dfull.at[:, :, my_d]
    cp = remote(half_d, half_d, dd_s, dd_r, partner)

    out_rows, out_cols = out.shape
    compact = n_slots * blk
    col_pos = lax.broadcasted_iota(jnp.int32, (out_cols, compact), 0) + o * out_cols
    row_i = lax.broadcasted_iota(jnp.int32, (n_hi * out_rows, compact), 0)
    row_pos = (row_i // out_rows * 2 + lo) * out_rows + lax.rem(row_i, out_rows)
    picks = []
    for l in range(2):
        where = jnp.concatenate([ids[l, s, 2:3, :] for s in range(n_occ)], axis=1)
        picks.append([(pos == where).astype(jnp.float32).astype(jnp.bfloat16) for pos in (col_pos, row_pos)])

    def spread(acc, l, i, t):
        for e in split(t):
            v = dot(picks[l][1][:, i * side:(i + 1) * side], e, NN)
            acc = v if acc is None else acc + v
        return acc

    cp.wait()
    acc = None
    for l in range(2):
        for i in range(n_y):
            dh, dl = split(dfull[l, i])
            cols = picks[l][0][:, i * side:(i + 1) * side]
            acc = spread(acc, l, i, dot(dh, cols, NT) + dot(dl, cols, NT))
    fwd = []
    for p in range(PIECES):
        oxs[p].wait()
        ref = ofull.at[1 - lo, pl.ds(pl.multiple_of(c * o_half + p * piece, piece), piece)]
        fwd.append(remote(ref, ref, of_s.at[p], of_r.at[p], partner))
    for cp in ops + fwd:
        cp.wait()
    for l in range(2):
        t = [None] * n_y
        for b, (i, k) in enumerate(offs):
            for e in split(ofull[l, b * side:(b + 1) * side, :]):
                vi = dot(e, picks[l][0][:, k * side:(k + 1) * side], NT)
                vk = dot(e, picks[l][0][:, i * side:(i + 1) * side], (((0,), (1,)), ((), ())))
                t[i] = vi if t[i] is None else t[i] + vi
                t[k] = vk if t[k] is None else t[k] + vk
        for i in range(n_y):
            acc = spread(acc, l, i, t[i])
    for h in range(n_hi):
        dense[h] = acc[h * out_rows:(h + 1) * out_rows, :]
    zs = []
    for d in range(1, n_hi):
        zs.append(remote(dense.at[lax.rem(hi_a + d, n_hi)], z_in.at[d - 1],
                         z_s.at[d - 1], z_r.at[d - 1], z_peer(d)))
    result = dense[hi_a]
    for d in range(1, n_hi):
        zs[d - 1].wait()
        result = result + z_in[d - 1]
    out[...] = result


def per_device(n_aux, n_occ, blocks, pair_list, pair_count, orbitals):
    n_q, slots, area = blocks.shape
    n_orb, nbf = orbitals.shape
    krows = area // LANES
    blk = 2 * krows
    tiles = blocks.reshape(n_q, slots, krows, LANES).transpose(0, 2, 1, 3).reshape(n_q, krows * slots, LANES)
    own_q = n_q // n_occ
    n_sub = 3
    sub_k = own_q // n_sub * n_orb
    compact = slots * n_occ * blk
    side = 2 * slots * blk
    n_y, n_hi = n_occ // 2, n_aux // 2
    off_rows = n_y * (n_y - 1) // 2 * side
    out_rows, out_cols = nbf // n_aux, nbf // n_occ
    f32, bf16, dma, vmem = jnp.float32, jnp.bfloat16, pltpu.SemaphoreType.DMA, pltpu.VMEM
    sems = [(n_y,)] + [(n_sub, n_occ)] * 2 + [(n_y,)] * 2 + [(n_occ - 1,)] * 2 + [()] * 6 + [(n_y,)] * 4
    sems += [()] * 4 + [(PIECES, n_y - 1)] * 2 + [(PIECES,)] * 6 + [(n_hi - 1,)] * 2
    return pl.pallas_call(
        functools.partial(kernel, n_aux, n_occ, n_sub),
        name="exchange",
        out_shape=jax.ShapeDtypeStruct((out_rows, out_cols), f32),
        in_specs=[pl.BlockSpec(memory_space=pl.ANY)] + [pl.BlockSpec(memory_space=pltpu.SMEM)] * 2
        + [pl.BlockSpec(memory_space=vmem)],
        out_specs=pl.BlockSpec(memory_space=vmem),
        scratch_shapes=[
            vmem((n_occ, own_q, krows * slots, LANES), f32),
            vmem((2, n_y - 1, own_q, krows * slots, LANES), f32),
            vmem((2, n_occ, 8, LANES), jnp.int32),
            vmem((slots * n_occ, 2 * n_orb, LANES), bf16),
            vmem((slots * n_occ, 2 * n_orb, LANES), bf16),
            vmem((compact, own_q * n_orb), bf16),
            vmem((compact, own_q * n_orb), bf16),
            vmem((side, sub_k), bf16),
            vmem((side, sub_k), bf16),
            vmem((side, side), f32),
            vmem((side // 2, side), f32),
            vmem((2, n_y, side, side), f32),
            vmem((off_rows, side), f32),
            vmem((off_rows // 2, side), f32),
            vmem((off_rows // 2, side), f32),
            vmem((n_y - 1, off_rows // 2, side), f32),
            vmem((2, off_rows, side), f32),
            vmem((n_hi, out_rows, out_cols), f32),
            vmem((n_hi - 1, out_rows, out_cols), f32),
        ] + [dma(s) for s in sems],
        compiler_params=pltpu.CompilerParams(collective_id=0, has_side_effects=True),
    )(tiles, pair_list, pair_count, orbitals)


def solution(mesh):
    body = functools.partial(per_device, mesh.shape["aux"], mesh.shape["occ"])
    in_specs = (P("aux", "occ", None), P("aux", "occ", None), P("aux"), P())
    return jax.shard_map(body, mesh=mesh, in_specs=in_specs, out_specs=P("aux", "occ"), check_vma=False)
```

time: 241 us -> 54.4 us (0.23)
  waiting for transfers between devices: 113 us -> 0 us
  Pallas kernels: 0 us -> 51.5 us
  matrix products: 43.9 us -> 0 us
  blocking collectives: 35.1 us -> 0 us
  local copies, waits for them, and re-layouts: 29 us -> 1.57 us
  between operations: 14.8 us -> 0.66 us
  starting transfers between devices: 4.43 us -> 0 us
    reduce_scatter x2 -> x0, waiting for transfers between devices: 113 us -> none  [the longest x1 89.5 us: per_device(): lax.psum_scatter(partial_value, 'aux', scatter_dimension=0, tiled=True)]
    pallas_call x0 -> x1, Pallas kernels: none -> 51.5 us  [per_device(): pl.pallas_call(functools.partial(kernel, n_aux, n_occ, n_sub), name='exch...]
    dot_general x4 -> x0, matrix products: 43.9 us -> none  [the longest x1 25 us: per_device(): jnp.einsum('rm,rn->mn', transformed, transformed, precision=lax.Precision...]
    unnamed x1 -> x0, blocking collectives: 35.1 us -> none
    reshape x4 -> x0, local copies, waits for them, and re-layouts: 24.2 us -> none  [the longest x1 11.6 us: per_device(): transformed = transformed.reshape(orbital_count // occ_devs * aux_rows, NBF)]
    all_to_all x1 -> x0, starting transfers between devices: 4.39 us -> none  [per_device(): lax.all_to_all(half_tiles.reshape(orbital_count, slot_count, aux_rows * B...]
  transfers between devices with their start and end apart: 3 -> 0, of which waited for: 2 -> 0; matrix products, arithmetic and copies ran while one was open for 0% -> 0% of each run, Pallas kernels for 0% -> 0%
where the time goes in v2:
time: 54.4 us; the launch traced here: 53.8 us
  Pallas kernels  51.5 us (95%)
  local copies, waits for them, and re-layouts  1.57 us (3%)
  between operations  0.66 us (1%)
    pallas_call x1, Pallas kernels, per_device(): pl.pallas_call(functools.partial(kernel, n_aux, n_occ, n_sub), name='exch...  51.5 us
    unnamed x1, local copies, waits for them, and re-layouts  1.57 us

profile of v2, /device:TPU:0, one launch (start us, length us, event | category | flops | bytes accessed | tf_op | source)
XLA Modules:
  0.0 53.8 jit_solution(14985514308797638439)
XLA Ops:
  0.7 51.5 %exchange.1 = f32[128,256]{1,0:T(8,128)} custom-call(f32[48,64,128]{2,1,0:T(8,128)} %bitcast.5, s32[1,2,2]{2,1,0:T(2,128)} %pairs_in.1, s32[1]{0:T(128)S(6)} %copy.7.count_in, f32[128,1024]{1,0:T(8,128)} %orb.1), custom_call_target="tpu_custom_call" | custom-call | tf_op jit(solution)/shard_map/exchange/pallas_call | solution.py:284
  52.2 1.6 %copy.8 = f32[128,256]{1,0:T(8,128)} copy(f32[128,256]{1,0:T(8,128)} %exchange.1) | data formatting | bytes 262144

commit v3 on v2

--- a/solution.py
+++ b/solution.py
@@ -1,4 +1,5 @@
 import functools
+import math
 
 import jax
 import jax.numpy as jnp
@@ -23,9 +24,9 @@
     return hi, (x - hi.astype(jnp.float32)).astype(jnp.bfloat16)
 
 
-def kernel(n_aux, n_occ, n_sub, tiles, pairs_in, count_in, orb, out, rx, rxd, ids, whi, wlo, hhi, hlo,
+def kernel(n_aux, n_occ, n_sub, tiles, pairs_hbm, count_in, orb_hbm, out, pairs_in, orb, rx, rxd, ids, whi, wlo, hhi, hlo,
            dhi, dlo, diag, dcore, dfull, off, ocore, opair, oin, ofull, dense, z_in,
-           local_s, tile_s, tile_r, quart_s, quart_r, ids_s, ids_r, idx_s, idx_r, dc_s, dc_r,
+           in_s, local_s, tile_s, tile_r, quart_s, quart_r, ids_s, ids_r, idx_s, idx_r, dc_s, dc_r,
            dx_s, dx_r, dy_s, dy_r, df_s, df_r, dd_s, dd_r, oc_s, oc_r, oy_s, oy_r, ox_s, ox_r,
            op_s, op_r, of_s, of_r, z_s, z_r):
     a, o = lax.axis_index("aux"), lax.axis_index("occ")
@@ -70,9 +71,32 @@
     def quarter(index):
         return tiles.at[pl.ds(index * own_q, own_q)]
 
+    inputs = [local(src, dst, in_s.at[n]) for n, (src, dst) in enumerate(
+        ((pairs_hbm, pairs_in), (orb_hbm, orb)))]
     locals_ = [local(quarter(o), rx.at[o], local_s.at[0])]
     for d in range(1, n_y):
         locals_.append(local(quarter(y_peer(d) * 2 + c), rxd.at[c, d - 1], local_s.at[d]))
+    pl.semaphore_wait(barrier, len(greet))
+
+    def remote(src, dst, s, r, dev):
+        cp = pltpu.make_async_remote_copy(
+            src_ref=src, dst_ref=dst, send_sem=s, recv_sem=r, device_id=dev, device_id_type=MESH
+        )
+        cp.start()
+        return cp
+
+    def sub_tiles(j, d, e):
+        peer = occ_peer(d, e)
+        n = d * 2 + e
+        return remote(tiles.at[pl.ds(peer * own_q + j * sub_q, sub_q)], rx.at[o, pl.ds(j * sub_q, sub_q)],
+                      tile_s.at[j, n], tile_r.at[j, n], (a, peer))
+
+    def tiles_of(j):
+        return [sub_tiles(j, d, e) for d in range(1, n_y) for e in (0, 1)]
+
+    tile_copies = [tiles_of(0)]
+    quarters = []
+    inputs[0].wait()
     lane1 = lax.broadcasted_iota(jnp.int32, (8, LANES), 1)
     row1 = lax.broadcasted_iota(jnp.int32, (8, LANES), 0)
     within = lax.rem(lane1, blk)
@@ -80,50 +104,39 @@
     live = [jnp.where(o * 2 + s < count_in[0], pairs_in[0, s, 0] * blk, -nbf - blk) for s in range(2)]
     cols = jnp.where(row1 == 0, pairs_in[0, 0, 1], pairs_in[0, 1, 1]) * blk + within
     ids[lo, o] = jnp.where(row1 < 2, cols, jnp.where(lane1 < blk, live[0], live[1]) + place)
-    pl.semaphore_wait(barrier, len(greet))
-
-    def remote(src, dst, s, r, dev):
-        cp = pltpu.make_async_remote_copy(
-            src_ref=src, dst_ref=dst, send_sem=s, recv_sem=r, device_id=dev, device_id_type=MESH
-        )
-        cp.start()
-        return cp
-
-    def sub_tiles(j, d, e):
-        peer = occ_peer(d, e)
-        n = d * 2 + e
-        return remote(tiles.at[pl.ds(peer * own_q + j * sub_q, sub_q)], rx.at[o, pl.ds(j * sub_q, sub_q)],
-                      tile_s.at[j, n], tile_r.at[j, n], (a, peer))
-
     id_copies = []
     for n, d in enumerate(peers):
         id_copies.append(remote(ids.at[lo, o], ids.at[lo, o], ids_s.at[n], ids_r.at[n], (a, occ_peer(*d))))
-    tile_copies = [[sub_tiles(j, d, e) for d in range(1, n_y) for e in (0, 1)] for j in range(n_sub)]
-    quarters = []
     for d in range(1, n_y):
         quarters.append(remote(quarter(y_peer(d) * 2 + 1 - c), rxd.at[c, d - 1],
                                quart_s.at[d], quart_r.at[d], partner))
     quarters.append(remote(quarter(o + 1 - 2 * c), rx.at[o], quart_s.at[0], quart_r.at[0], partner))
-
+    for j in range(1, n_sub):
+        tile_copies.append(tiles_of(j))
+    inputs[1].wait()
     orb_hi, orb_lo = split(orb[...])
     row_pos = lax.broadcasted_iota(jnp.int32, (nbf, LANES), 0)
     lane = lax.broadcasted_iota(jnp.int32, (n_orb, LANES), 1)
-    for cp in id_copies:
-        cp.wait()
-    idx_copy = remote(ids.at[lo], ids.at[lo], idx_s, idx_r, x_peer)
-    for s in range(n_slots):
-        sel = (row_pos == ids[lo, s // 2, pl.ds(s % 2, 1), :]).astype(jnp.float32)
-        sel = sel.astype(jnp.bfloat16)
-        for src, dst in ((orb_hi, whi), (orb_lo, wlo)):
-            w = dot(src, sel, NN)
-            dst[s, 0:n_orb, :] = jnp.where(lane < blk, w, 0.0).astype(jnp.bfloat16)
-            dst[s, n_orb:2 * n_orb, :] = jnp.where(lane >= blk, w, 0.0).astype(jnp.bfloat16)
+    def weights(src):
+        for s in range(2):
+            sel = (row_pos == ids[lo, src, pl.ds(s, 1), :]).astype(jnp.float32).astype(jnp.bfloat16)
+            for orb_part, copies, dst in ((orb_hi, 2, whi), (orb_lo, 1, wlo)):
+                w = dot(orb_part, sel, NN)
+                for p in range(2):
+                    keep = lane < blk if p == 0 else lane >= blk
+                    w_p = jnp.where(keep, w, 0.0).astype(jnp.bfloat16)
+                    for n in range(copies):
+                        dst[src * 2 + s, p * n_orb:(p + 1) * n_orb, n * LANES:(n + 1) * LANES] = w_p
+
+    id_copies[-1].wait()
+    for e in range(2):
+        weights(y * 2 + e)
 
     def half(load, slot, row0, q0, hi_ref, lo_ref):
         rows = jnp.concatenate([load(q) for q in range(sub_q)], axis=0)
         bh, bl = split(rows)
         wh, wl = whi[slot], wlo[slot]
-        res = dot(bh, wh, NT) + dot(bl, wh, NT) + dot(bh, wl, NT)
+        res = dot(jnp.concatenate([bh, bl], axis=1), wh, NT) + dot(bh, wl, NT)
         for q in range(sub_q):
             for p in range(2):
                 ph, pl_ = split(res[q * krows:(q + 1) * krows, p * n_orb:(p + 1) * n_orb])
@@ -162,6 +175,12 @@
     dx = [remote(my_diag, my_diag, dx_s, dx_r, x_peer)]
     dys = [remote(my_diag, my_diag, dy_s.at[d], dy_r.at[d], (a, y_peer(d) * 2 + c)) for d in range(1, n_y)]
 
+    for cp in id_copies[:-1]:
+        cp.wait()
+    idx_copy = remote(ids.at[lo], ids.at[lo], idx_s, idx_r, x_peer)
+    for d in range(1, n_y):
+        for e in range(2):
+            weights(y_peer(d) * 2 + e)
     offs = [(i, k) for i in range(n_y) for k in range(i)]
     for j in range(n_sub):
         for cp in tile_copies[j]:
@@ -211,11 +230,12 @@
     half_d = dfull.at[:, :, my_d]
     cp = remote(half_d, half_d, dd_s, dd_r, partner)
 
-    out_rows, out_cols = out.shape
+    out_rows, out_cols = out.shape[1:]
     compact = n_slots * blk
     col_pos = lax.broadcasted_iota(jnp.int32, (out_cols, compact), 0) + o * out_cols
     row_i = lax.broadcasted_iota(jnp.int32, (n_hi * out_rows, compact), 0)
-    row_pos = (row_i // out_rows * 2 + lo) * out_rows + lax.rem(row_i, out_rows)
+    row_h = lax.rem(row_i // out_rows + 1 + hi_a, n_hi)
+    row_pos = (row_h * 2 + lo) * out_rows + lax.rem(row_i, out_rows)
     picks = []
     for l in range(2):
         where = jnp.concatenate([ids[l, s, 2:3, :] for s in range(n_occ)], axis=1)
@@ -241,6 +261,7 @@
         fwd.append(remote(ref, ref, of_s.at[p], of_r.at[p], partner))
     for cp in ops + fwd:
         cp.wait()
+    parts = []
     for l in range(2):
         t = [None] * n_y
         for b, (i, k) in enumerate(offs):
@@ -249,19 +270,27 @@
                 vk = dot(e, picks[l][0][:, i * side:(i + 1) * side], (((0,), (1,)), ((), ())))
                 t[i] = vi if t[i] is None else t[i] + vi
                 t[k] = vk if t[k] is None else t[k] + vk
-        for i in range(n_y):
-            acc = spread(acc, l, i, t[i])
-    for h in range(n_hi):
-        dense[h] = acc[h * out_rows:(h + 1) * out_rows, :]
+        parts.append([split(v) for v in t])
     zs = []
-    for d in range(1, n_hi):
-        zs.append(remote(dense.at[lax.rem(hi_a + d, n_hi)], z_in.at[d - 1],
-                         z_s.at[d - 1], z_r.at[d - 1], z_peer(d)))
-    result = dense[hi_a]
+    for g in range(n_hi // 2):
+        rows = slice(2 * g * out_rows, 2 * (g + 1) * out_rows)
+        v = acc[rows, :]
+        for l in range(2):
+            for i in range(n_y):
+                for e in parts[l][i]:
+                    v = v + dot(picks[l][1][rows, i * side:(i + 1) * side], e, NN)
+        for n in range(2):
+            d = 2 * g + n + 1
+            if d < n_hi:
+                dense[d - 1] = v[n * out_rows:(n + 1) * out_rows, :]
+                zs.append(remote(dense.at[d - 1], z_in.at[d - 1], z_s.at[d - 1], z_r.at[d - 1], z_peer(d)))
+            else:
+                out[0] = v[n * out_rows:(n + 1) * out_rows, :]
+    result = None
     for d in range(1, n_hi):
         zs[d - 1].wait()
-        result = result + z_in[d - 1]
-    out[...] = result
+        result = z_in[d - 1] if result is None else result + z_in[d - 1]
+    out[1] = result
 
 
 def per_device(n_aux, n_occ, blocks, pair_list, pair_count, orbitals):
@@ -271,7 +300,7 @@
     blk = 2 * krows
     tiles = blocks.reshape(n_q, slots, krows, LANES).transpose(0, 2, 1, 3).reshape(n_q, krows * slots, LANES)
     own_q = n_q // n_occ
-    n_sub = 3
+    n_sub = math.gcd(own_q, 6)
     sub_k = own_q // n_sub * n_orb
     compact = slots * n_occ * blk
     side = 2 * slots * blk
@@ -279,20 +308,21 @@
     off_rows = n_y * (n_y - 1) // 2 * side
     out_rows, out_cols = nbf // n_aux, nbf // n_occ
     f32, bf16, dma, vmem = jnp.float32, jnp.bfloat16, pltpu.SemaphoreType.DMA, pltpu.VMEM
-    sems = [(n_y,)] + [(n_sub, n_occ)] * 2 + [(n_y,)] * 2 + [(n_occ - 1,)] * 2 + [()] * 6 + [(n_y,)] * 4
+    sems = [(2,), (n_y,)] + [(n_sub, n_occ)] * 2 + [(n_y,)] * 2 + [(n_occ - 1,)] * 2 + [()] * 6 + [(n_y,)] * 4
     sems += [()] * 4 + [(PIECES, n_y - 1)] * 2 + [(PIECES,)] * 6 + [(n_hi - 1,)] * 2
-    return pl.pallas_call(
+    sums = pl.pallas_call(
         functools.partial(kernel, n_aux, n_occ, n_sub),
         name="exchange",
-        out_shape=jax.ShapeDtypeStruct((out_rows, out_cols), f32),
-        in_specs=[pl.BlockSpec(memory_space=pl.ANY)] + [pl.BlockSpec(memory_space=pltpu.SMEM)] * 2
-        + [pl.BlockSpec(memory_space=vmem)],
+        out_shape=jax.ShapeDtypeStruct((2, out_rows, out_cols), f32),
+        in_specs=[pl.BlockSpec(memory_space=space) for space in (pl.ANY, pl.ANY, pltpu.SMEM, pl.ANY)],
         out_specs=pl.BlockSpec(memory_space=vmem),
         scratch_shapes=[
+            pltpu.SMEM(pair_list.shape, jnp.int32),
+            vmem(orbitals.shape, f32),
             vmem((n_occ, own_q, krows * slots, LANES), f32),
             vmem((2, n_y - 1, own_q, krows * slots, LANES), f32),
             vmem((2, n_occ, 8, LANES), jnp.int32),
-            vmem((slots * n_occ, 2 * n_orb, LANES), bf16),
+            vmem((slots * n_occ, 2 * n_orb, 2 * LANES), bf16),
             vmem((slots * n_occ, 2 * n_orb, LANES), bf16),
             vmem((compact, own_q * n_orb), bf16),
             vmem((compact, own_q * n_orb), bf16),
@@ -306,11 +336,12 @@
             vmem((off_rows // 2, side), f32),
             vmem((n_y - 1, off_rows // 2, side), f32),
             vmem((2, off_rows, side), f32),
-            vmem((n_hi, out_rows, out_cols), f32),
+            vmem((n_hi - 1, out_rows, out_cols), f32),
             vmem((n_hi - 1, out_rows, out_cols), f32),
         ] + [dma(s) for s in sems],
         compiler_params=pltpu.CompilerParams(collective_id=0, has_side_effects=True),
     )(tiles, pair_list, pair_count, orbitals)
+    return sums[0] + sums[1]
 
 
 def solution(mesh):

time: 54.4 us -> 53.1 us (0.976)
  other arithmetic: 0 us -> 1.64 us
  local copies, waits for them, and re-layouts: 1.57 us -> 0 us
  Pallas kernels: 51.5 us -> 50.2 us
    add x0 -> x1, other arithmetic: none -> 1.64 us  [per_device(): return sums[0] + sums[1]]
    unnamed x1 -> x0, local copies, waits for them, and re-layouts: 1.57 us -> none
    pallas_call x1, Pallas kernels: 51.5 us -> 50.2 us  [per_device(): pl.pallas_call(functools.partial(kernel, n_aux, n_occ, n_sub), name='exch...]
where the time goes in v3:
time: 53.1 us; the launch traced here: 52.5 us
  Pallas kernels  50.2 us (95%)
  other arithmetic  1.64 us (3%)
  between operations  0.66 us (1%)
    pallas_call x1, Pallas kernels, per_device(): pl.pallas_call(functools.partial(kernel, n_aux, n_occ, n_sub), name='exch...  50.2 us
    add x1, other arithmetic, per_device(): return sums[0] + sums[1]  1.64 us

profile of v3, /device:TPU:0, one launch (start us, length us, event | category | flops | bytes accessed | tf_op | source)
XLA Modules:
  0.0 52.5 jit_solution(16635294252218524931)
XLA Ops:
  0.7 50.2 %exchange.1 = f32[2,128,256]{2,1,0:T(8,128)} custom-call(f32[48,64,128]{2,1,0:T(8,128)} %bitcast.7, s32[1,2,2]{2,1,0:T(2,128)} %pairs_hbm.1, s32[1]{0:T(128)S(6)} %copy.6.count_in, f32[128,1024]{1,0:T(8,128)} %orb_hbm.1), custom_call_target="tpu_custom_call" | custom-call | tf_op jit(solution)/shard_map/exchange/pallas_call | solution.py:313
  50.8 1.6 %add_bitcast_fusion = f32[128,256]{1,0:T(8,128)} fusion(f32[2,128,256]{2,1,0:T(8,128)} %exchange.1), kind=kLoop, calls=%fused_computation | loop fusion | flops 32768 | bytes 393216 | tf_op jit(solution)/shard_map/add | solution.py:344
